TPU v7x, 32 devices: a whole 2x2x4 slice. The times are simulated.
32 devices in a mesh: groups: 2 (over y), row: 8 (over z, x), col: 2 (over core).
Axes of the slice: x: 2, y: 2, z: 4, core: 2. Of those that a mesh axis runs over, the one named last changes fastest.
Arguments:
- embeddings: bfloat16 [128, 16, 1280], P(('groups', 'row'), 'col'), parts along dimension 0, may hold values from -6 to 52
- pos_embed: bfloat16 [256, 1280], replicated, may hold values from -3 to 3
- ln_gain: float32 [1280], replicated, may hold values from 0.6 to 9
- ln_bias: float32 [1280], replicated, may hold values from -1.5 to 1.5
- w_qkv: bfloat16 [1280, 1920], P(('row', 'col')), may hold values from -0.25155765 to 0.25155765
- b_qkv: float32 [1920], replicated, may hold values from -1.5 to 1.5
- w_out: bfloat16 [1280, 640], P(('row', 'col')), may hold values from -0.25 to 0.25
- b_out: float32 [1280], replicated, may hold values from -1.5 to 1.5
- valid: int32 [16, 2, 256], P(('groups', 'row'), 'col'), parts along dimension 0, may hold values from 0 to 196
Outputs:
- merged: bfloat16 [128, 16, 1280], P(('groups', 'row'), 'col'), parts along dimension 0
There are 2 independent parts, one for each index of `groups`. A program takes and returns all parts, laid end to end along the dimension named above; an argument that names none is the same for every part. Nothing has to cross between parts.
All inputs are finite; a program needn't handle non-finite values.
Results may differ from a plain program's by a relative error of at most 0.0098.
Values may be sent and summed in bfloat16 or wider, within the bound.
A program may use at most 64 MiB of HBM per device.

v0:
```python
import jax
import jax.numpy as jnp
from jax import lax
from jax.sharding import PartitionSpec as P

HEADS = 8
EPSILON = 1e-06
SPREAD = 4.0
FLOOR = 0.25


def shifted(value, axis, steps):
    count = lax.axis_size(axis)
    initial, last = (max(0, -steps), min(count, count - steps))
    return lax.ppermute(value, axis, [(source, source + steps) for source in range(initial, last)])


def extended(block, sides, width):
    for axis, dim in sides:
        count = lax.axis_size(axis)
        forward = [(i, i + 1) for i in range(count - 1)]
        backward = [(target, source) for source, target in forward]
        low = lax.ppermute(
            lax.slice_in_dim(block, block.shape[dim] - width, None, axis=dim), axis, forward
        )
        high = lax.ppermute(lax.slice_in_dim(block, 0, width, axis=dim), axis, backward)
        block = jnp.concatenate([low, block, high], axis=dim)
    return block


def layer_norm(inputs, ln_gain, ln_bias):
    centred = inputs - jnp.mean(inputs, axis=-1, keepdims=True)
    variance = jnp.mean(centred * centred, axis=-1, keepdims=True)
    return centred * lax.rsqrt(variance + EPSILON) * ln_gain + ln_bias


def gauss_table(win):
    offsets = jnp.arange(win, dtype=jnp.float32) - (win - 1) / 2.0
    squared = offsets[:, None] * offsets[:, None] + offsets[None, :] * offsets[None, :]
    return jnp.exp(-squared / (2.0 * SPREAD * SPREAD))


def attend(projected):
    rows_count = projected.shape[0]
    width = projected.shape[1] // 3
    head_size = width // HEADS
    queries = projected[:, :width].reshape(rows_count, HEADS, head_size)
    keys = projected[:, width : 2 * width].reshape(rows_count, HEADS, head_size)
    values = projected[:, 2 * width :].reshape(rows_count, HEADS, head_size)
    scores = jnp.einsum(
        "qhd,khd->hqk", queries, keys, preferred_element_type=jnp.float32
    ) * head_size ** (-0.5)
    highest = jnp.max(scores, axis=-1, keepdims=True)
    expon = jnp.exp(scores - highest)
    probs = (expon / jnp.sum(expon, axis=-1, keepdims=True)).astype(jnp.bfloat16)
    mixed = jnp.einsum("hqk,khd->qhd", probs, values, preferred_element_type=jnp.float32)
    return mixed.astype(jnp.bfloat16).reshape(rows_count, width)


def fold_rows(numerator, denominator, rim):
    from_next = (
        shifted(numerator[:rim].astype(jnp.bfloat16), "row", -1).astype(jnp.float32),
        shifted(denominator[:rim].astype(jnp.bfloat16), "row", -1).astype(jnp.float32),
    )
    from_prev = (
        shifted(numerator[-rim:].astype(jnp.bfloat16), "row", 1).astype(jnp.float32),
        shifted(denominator[-rim:].astype(jnp.bfloat16), "row", 1).astype(jnp.float32),
    )
    middle_num = numerator[rim:-rim]
    middle_den = denominator[rim:-rim]
    middle_num = middle_num.at[:rim].add(from_prev[0]).at[-rim:].add(from_next[0])
    middle_den = middle_den.at[:rim].add(from_prev[1]).at[-rim:].add(from_next[1])
    return (middle_num, middle_den)


def fold_cols(numerator, denominator, rim):
    from_next = (
        shifted(numerator[:, :rim].astype(jnp.bfloat16), "col", -1).astype(jnp.float32),
        shifted(denominator[:, :rim].astype(jnp.bfloat16), "col", -1).astype(jnp.float32),
    )
    from_prev = (
        shifted(numerator[:, -rim:].astype(jnp.bfloat16), "col", 1).astype(jnp.float32),
        shifted(denominator[:, -rim:].astype(jnp.bfloat16), "col", 1).astype(jnp.float32),
    )
    middle_num = numerator[:, rim:-rim] + jnp.concatenate([from_prev[0], from_next[0]], axis=1)
    middle_den = denominator[:, rim:-rim] + jnp.concatenate([from_prev[1], from_next[1]], axis=1)
    return (middle_num, middle_den)


def body(embeddings, pos_embed, ln_gain, ln_bias, w_qkv, b_qkv, w_out, b_out, valid):
    tile = embeddings.shape[1]
    tile_rows = embeddings.shape[0] // tile
    rim = tile // 2
    win = tile + 2 * rim
    rows_count = win * win
    width_model = embeddings.shape[2]
    window = extended(embeddings, (("row", 0), ("col", 1)), rim)
    stacked = jnp.stack([window], axis=0)
    inputs = stacked.reshape(tile_rows, rows_count, width_model).astype(
        jnp.float32
    ) + pos_embed.astype(jnp.float32)
    inputs = inputs.reshape(tile_rows * rows_count, width_model)
    normed = layer_norm(inputs, ln_gain, ln_bias).astype(jnp.bfloat16)
    projected = jnp.dot(
        normed,
        lax.all_gather(w_qkv, ("row", "col"), axis=0, tiled=True),
        preferred_element_type=jnp.float32,
    )
    projected = (
        (projected + b_qkv).astype(jnp.bfloat16).reshape(tile_rows, rows_count, w_qkv.shape[1])
    )
    attended = jax.vmap(attend)(projected).reshape(tile_rows * rows_count, -1)
    projected_out = lax.dot_general(
        attended,
        lax.all_gather(w_out, ("row", "col"), axis=0, tiled=True),
        (((1,), (1,)), ((), ())),
        preferred_element_type=jnp.float32,
    )
    hidden = inputs + projected_out + b_out
    gauss = gauss_table(win).reshape(1, rows_count)
    weight = gauss * valid.reshape(tile_rows, rows_count).astype(jnp.float32) / 196.0
    contrib = (weight.reshape(tile_rows * rows_count, 1) * hidden).reshape(
        tile_rows, win, win, width_model
    )
    weight_grid = weight.reshape(tile_rows, win, win)
    numerator = jnp.zeros((tile_rows * tile + 2 * rim, win, width_model), jnp.float32)
    denominator = jnp.zeros((tile_rows * tile + 2 * rim, win), jnp.float32)
    numerator = numerator.at[0:win].add(contrib[0])
    denominator = denominator.at[0:win].add(weight_grid[0])
    numerator, denominator = fold_rows(numerator, denominator, rim)
    numerator, denominator = fold_cols(numerator, denominator, rim)
    return (numerator / jnp.maximum(denominator, FLOOR)[:, :, None]).astype(jnp.bfloat16)


def solution(mesh):
    placed = (
        P(("groups", "row"), "col", None),
        P(),
        P(),
        P(),
        P(("row", "col"), None),
        P(),
        P(("row", "col"), None),
        P(),
        P(("groups", "row"), "col", None),
    )
    return jax.shard_map(
        body,
        mesh=mesh,
        in_specs=placed,
        out_specs=P(("groups", "row"), "col", None),
        check_vma=False,
    )
```

profile of v0, /device:TPU:0, one launch (start us, length us, event | category | flops | bytes accessed | tf_op | source)
XLA Modules:
  0.0 136.9 jit_solution(5850899575125565786)
XLA Ops:
  7.3 0.9 fusion.25
  8.2 4.9 %collective-permute-start = (bf16[4,8,1280]{2,1,0:T(8,128)(2,1)S(1)}, bf16[4,8,1280]{2,1,0:T(8,128)(2,1)S(1)}, u32[]{:S(2)}, u32[]{:S(2)}) collective-permute-start(bf16[4,8,1280]{2,1,0:T(8,128)(2,1)S(1)} %get-tuple-element.105), channel_id=1, source_target_pairs={{0,2},{2,4},{4,6},{6,8},{8,10},{10,12},{12,14},{1,3},{3,5},{5,7},{... | collective-permute-start | bytes 245768 | tf_op jit(solution)/shard_map/ppermute | solution.py:23
  13.1 1.3 collective-permute-start.1
  15.3 4.5 %collective-permute-start.8 = (bf16[4,16]{1,0:T(4,128)(2,1)S(1)}, bf16[4,16]{1,0:T(4,128)(2,1)S(1)}, u32[]{:S(2)}, u32[]{:S(2)}) collective-permute-start(bf16[4,16]{1,0:T(4,128)(2,1)S(1)} %get-tuple-element.107), channel_id=1, source_target_pairs={{0,2},{2,4},{4,6},{6,8},{8,10},{10,12},{12,14},{1,3},{3,5},{5,7},{... | collective-permute-start | bytes 392 | tf_op jit(solution)/shard_map/ppermute | solution.py:15
  19.9 1.3 collective-permute-start.9
  22.1 1.0 constant_dynamic-update-slice_fusion.1
  23.2 1.3 collective-permute-start.2
  24.6 1.3 collective-permute-start.3
  25.9 1.9 %collective-permute-done.3 = bf16[16,4,1280]{2,1,0:T(4,128)(2,1)S(1)} collective-permute-done((bf16[16,4,1280]{2,1,0:T(4,128)(2,1)S(1)}, bf16[16,4,1280]{2,1,0:T(4,128)(2,1)S(1)}, u32[]{:S(2)}, u32[]{:S(2)}) %collective-permute-start.3) | collective-permute-done | bytes 163872 | tf_op jit(solution)/shard_map/ppermute | solution.py:26
  28.9 37.5 %all-gather.3.cloned.1.call-done = bf16[1280,1920]{1,0:T(8,128)(2,1)} async-done(((bf16[80,1920]{1,0:T(8,128)(2,1)}), bf16[1280,1920]{1,0:T(8,128)(2,1)}) %all-gather.3.cloned.1.call-update) | async-done | bytes 4915216 | tf_op jit(solution)/shard_map/all_gather | solution.py:106
  66.4 4.1 %fusion.4 = bf16[1,256,1920]{2,1,0:T(8,128)(2,1)S(1)} fusion(bf16[1280,1920]{1,0:T(8,128)(2,1)} %all-gather.3.cloned.1.call-done, f32[1920]{0:T(1024)S(1)} %copy-done.2, bf16[256,1280]{1,0:T(8,128)(2,1)S(1)} %copy-done, bf16[256,1280]{1,0:T(8,128)(2,1)S(1)} %bitcast.37, f32[1280]{0:T(1024)S(1)} %copy-done.3, f32[1280]{0:T(1024)S(1)} %copy-done.4, ...), kind=kOutput, calls=%fused_computation.6 | convolution fusion | flops 1261895680 | bytes 7228928 | tf_op jit(solution)/shard_map/dot_general | solution.py:104
  71.2 2.2 %fusion.27 = (f32[8,256]{1,0:T(8,128)S(1)}, f32[8,256,256]{1,2,0:T(8,128)}) fusion(bf16[256,8,80]{0,2,1:T(8,128)(2,1)S(1)} %bitcast.42, bf16[256,8,80]{0,2,1:T(8,128)(2,1)S(1)} %bitcast.43), kind=kOutput, calls=%fused_computation.55 | convolution fusion | flops 85459200 | bytes 2760704 | tf_op jit(solution)/shard_map/vmap()/sub | solution.py:54
  73.3 2.0 %convolution_convert_fusion = bf16[8,80,256]{2,1,0:T(8,128)(2,1)S(1)} fusion(bf16[256,8,80]{0,2,1:T(8,128)(2,1)S(1)} %bitcast.44, f32[8,256,256]{1,2,0:T(8,128)} %get-tuple-element.111, f32[8,256]{1,0:T(8,128)S(1)} %get-tuple-element.110), kind=kOutput, calls=%fused_computation.14 | convolution fusion | flops 85098496 | bytes 2760704 | tf_op jit(solution)/shard_map/vmap(hqk,khd->qhd)/dot_general | solution.py:56
  75.3 31.7 %all-gather.5.cloned.1.call-done = bf16[1280,640]{1,0:T(8,128)(2,1)} async-done(((bf16[80,640]{1,0:T(8,128)(2,1)}), bf16[1280,640]{1,0:T(8,128)(2,1)}) %all-gather.5.cloned.1.call-update) | async-done | bytes 1638416 | tf_op jit(solution)/shard_map/all_gather | solution.py:115
  107.0 2.3 %fusion.28 = (bf16[256,1280]{1,0:T(8,128)(2,1)S(1)}, f32[256,1280]{1,0:T(8,128)S(1)}) fusion(f32[1280]{0:T(1024)S(1)} %copy-done.1, bf16[256,640]{0,1:T(8,128)(2,1)S(1)} %bitcast.41, bf16[1280,640]{1,0:T(8,128)(2,1)} %all-gather.5.cloned.1.call-done, bf16[256,1280]{1,0:T(8,128)(2,1)S(1)} %copy-done, bf16[256,1280]{1,0:T(8,128)(2,1)S(1)} %bitcast.38, ...), kind=kOutput, calls=%fused_computation.56 | convolution fusion | flops 421724160 | bytes 5249024 | tf_op jit(solution)/shard_map/dot_general | solution.py:113
  109.3 2.4 %collective-permute-start.4 = (bf16[4,16,1280]{2,1,0:T(8,128)(2,1)S(1)}, bf16[4,16,1280]{2,1,0:T(8,128)(2,1)S(1)}, u32[]{:S(2)}, u32[]{:S(2)}) collective-permute-start(bf16[4,16,1280]{2,1,0:T(8,128)(2,1)S(1)} %bitcast.46), channel_id=1, source_target_pairs={{0,2},{2,4},{4,6},{6,8},{8,10},{10,12},{12,14},{1,3},{3,5},{5,7},{... | collective-permute-start | bytes 491528 | tf_op jit(solution)/shard_map/ppermute | solution.py:15
  111.8 1.8 %collective-permute-start.10 = (bf16[8,4]{1,0:T(8,128)(2,1)S(1)}, bf16[8,4]{1,0:T(8,128)(2,1)S(1)}, u32[]{:S(2)}, u32[]{:S(2)}) collective-permute-start(bf16[8,4]{1,0:T(8,128)(2,1)S(1)} %get-tuple-element.108), channel_id=1, source_target_pairs={{0,1},{2,3},{4,5},{6,7},{8,9},{10,11},{12,13},{14,15},{16,17},{18,... | collective-permute-start | bytes 200 | tf_op jit(solution)/shard_map/ppermute | solution.py:15
  113.6 1.3 collective-permute-start.11
  115.0 1.3 collective-permute-start.5
  116.4 7.5 %collective-permute-done.5 = bf16[4,16,1280]{2,1,0:T(8,128)(2,1)S(1)} collective-permute-done((bf16[4,16,1280]{2,1,0:T(8,128)(2,1)S(1)}, bf16[4,16,1280]{2,1,0:T(8,128)(2,1)S(1)}, u32[]{:S(2)}, u32[]{:S(2)}) %collective-permute-start.5) | collective-permute-done | bytes 163872 | tf_op jit(solution)/shard_map/ppermute | solution.py:15
  124.0 2.0 %collective-permute-start.6 = (bf16[8,4,1280]{2,1,0:T(4,128)(2,1)S(1)}, bf16[8,4,1280]{2,1,0:T(4,128)(2,1)S(1)}, u32[]{:S(2)}, u32[]{:S(2)}) collective-permute-start(bf16[8,4,1280]{2,1,0:T(4,128)(2,1)S(1)} %get-tuple-element.100), channel_id=1, source_target_pairs={{0,1},{2,3},{4,5},{6,7},{8,9},{10,11},{12,13},{14,15},{16,17},{18,... | collective-permute-start | bytes 245768 | tf_op jit(solution)/shard_map/ppermute | solution.py:15
  126.1 1.3 collective-permute-start.7
  127.5 1.8 %collective-permute-done.7 = bf16[8,4,1280]{2,1,0:T(4,128)(2,1)S(1)} collective-permute-done((bf16[8,4,1280]{2,1,0:T(4,128)(2,1)S(1)}, bf16[8,4,1280]{2,1,0:T(4,128)(2,1)S(1)}, u32[]{:S(2)}, u32[]{:S(2)}) %collective-permute-start.7) | collective-permute-done | bytes 81952 | tf_op jit(solution)/shard_map/ppermute | solution.py:15
  129.2 0.8 fusion.13
  (57 shorter events, 4.8 us)
Async XLA Ops:
  6.5 59.8 %all-gather.3.cloned.1.call-start = ((), (), s32[]{:S(2)}) async-start(), calls=%async_computation | async-start | bytes 5222400 | tf_op jit(solution)/shard_map/all_gather | solution.py:106
  7.3 99.8 %all-gather.5.cloned.1.call-start = ((), (), s32[]{:S(2)}) async-start(), calls=%async_computation.1 | async-start | bytes 1740800 | tf_op jit(solution)/shard_map/all_gather | solution.py:115
  8.2 13.8 %collective-permute-start = (bf16[4,8,1280]{2,1,0:T(8,128)(2,1)S(1)}, bf16[4,8,1280]{2,1,0:T(8,128)(2,1)S(1)}, u32[]{:S(2)}, u32[]{:S(2)}) collective-permute-start(bf16[4,8,1280]{2,1,0:T(8,128)(2,1)S(1)} %get-tuple-element.105), channel_id=1, source_target_pairs={{0,2},{2,4},{4,6},{6,8},{8,10},{10,12},{12,14},{1,3},{3,5},{5,7},{... | collective-permute-start | bytes 245768 | tf_op jit(solution)/shard_map/ppermute | solution.py:23
  13.1 10.0 %collective-permute-start.1 = (bf16[4,8,1280]{2,1,0:T(8,128)(2,1)S(1)}, bf16[4,8,1280]{2,1,0:T(8,128)(2,1)S(1)}, u32[]{:S(2)}, u32[]{:S(2)}) collective-permute-start(bf16[4,8,1280]{2,1,0:T(8,128)(2,1)S(1)} %get-tuple-element.104), channel_id=1, source_target_pairs={{2,0},{4,2},{6,4},{8,6},{10,8},{12,10},{14,12},{3,1},{5,3},{7,5},{... | collective-permute-start | bytes 245768 | tf_op jit(solution)/shard_map/ppermute | solution.py:26
  15.3 6.7 %collective-permute-start.8 = (bf16[4,16]{1,0:T(4,128)(2,1)S(1)}, bf16[4,16]{1,0:T(4,128)(2,1)S(1)}, u32[]{:S(2)}, u32[]{:S(2)}) collective-permute-start(bf16[4,16]{1,0:T(4,128)(2,1)S(1)} %get-tuple-element.107), channel_id=1, source_target_pairs={{0,2},{2,4},{4,6},{6,8},{8,10},{10,12},{12,14},{1,3},{3,5},{5,7},{... | collective-permute-start | bytes 392 | tf_op jit(solution)/shard_map/ppermute | solution.py:15
  19.9 6.0 %collective-permute-start.9 = (bf16[4,16]{1,0:T(4,128)(2,1)S(1)}, bf16[4,16]{1,0:T(4,128)(2,1)S(1)}, u32[]{:S(2)}, u32[]{:S(2)}) collective-permute-start(bf16[4,16]{1,0:T(4,128)(2,1)S(1)} %get-tuple-element.106), channel_id=1, source_target_pairs={{2,0},{4,2},{6,4},{8,6},{10,8},{12,10},{14,12},{3,1},{5,3},{7,5},{... | collective-permute-start | bytes 392 | tf_op jit(solution)/shard_map/ppermute | solution.py:15
  22.1 6.1 %copy-start = (bf16[256,1280]{1,0:T(8,128)(2,1)S(1)}, bf16[256,1280]{1,0:T(8,128)(2,1)}, u32[]{:S(2)}) copy-start(bf16[256,1280]{1,0:T(8,128)(2,1)} %param.26) | copy-start | bytes 1966084
  23.2 2.7 %collective-permute-start.2 = (bf16[16,4,1280]{2,1,0:T(4,128)(2,1)S(1)}, bf16[16,4,1280]{2,1,0:T(4,128)(2,1)S(1)}, u32[]{:S(2)}, u32[]{:S(2)}) collective-permute-start(bf16[16,4,1280]{2,1,0:T(4,128)(2,1)S(1)} %get-tuple-element.102), channel_id=1, source_target_pairs={{0,1},{2,3},{4,5},{6,7},{8,9},{10,11},{12,13},{14,15},{16,17},{18,... | collective-permute-start | bytes 491528 | tf_op jit(solution)/shard_map/ppermute | solution.py:23
  24.6 3.3 %collective-permute-start.3 = (bf16[16,4,1280]{2,1,0:T(4,128)(2,1)S(1)}, bf16[16,4,1280]{2,1,0:T(4,128)(2,1)S(1)}, u32[]{:S(2)}, u32[]{:S(2)}) collective-permute-start(bf16[16,4,1280]{2,1,0:T(4,128)(2,1)S(1)} %get-tuple-element.103), channel_id=1, source_target_pairs={{1,0},{3,2},{5,4},{7,6},{9,8},{11,10},{13,12},{15,14},{17,16},{19,... | collective-permute-start | bytes 491528 | tf_op jit(solution)/shard_map/ppermute | solution.py:26
  28.2 38.2 %copy-start.2 = (f32[1920]{0:T(1024)S(1)}, f32[1920]{0:T(1024)}, u32[]{:S(2)}) copy-start(f32[1920]{0:T(1024)} %param.30) | copy-start | bytes 23044
  28.2 38.2 %copy-start.3 = (f32[1280]{0:T(1024)S(1)}, f32[1280]{0:T(1024)}, u32[]{:S(2)}) copy-start(f32[1280]{0:T(1024)} %param.28) | copy-start | bytes 15364
  28.2 38.2 %copy-start.4 = (f32[1280]{0:T(1024)S(1)}, f32[1280]{0:T(1024)}, u32[]{:S(2)}) copy-start(f32[1280]{0:T(1024)} %param.27) | copy-start | bytes 15364
  73.3 33.7 %copy-start.1 = (f32[1280]{0:T(1024)S(1)}, f32[1280]{0:T(1024)}, u32[]{:S(2)}) copy-start(f32[1280]{0:T(1024)} %param.32) | copy-start | bytes 15364
  109.3 7.0 %collective-permute-start.4 = (bf16[4,16,1280]{2,1,0:T(8,128)(2,1)S(1)}, bf16[4,16,1280]{2,1,0:T(8,128)(2,1)S(1)}, u32[]{:S(2)}, u32[]{:S(2)}) collective-permute-start(bf16[4,16,1280]{2,1,0:T(8,128)(2,1)S(1)} %bitcast.46), channel_id=1, source_target_pairs={{0,2},{2,4},{4,6},{6,8},{8,10},{10,12},{12,14},{1,3},{3,5},{5,7},{... | collective-permute-start | bytes 491528 | tf_op jit(solution)/shard_map/ppermute | solution.py:15
  111.8 15.6 %collective-permute-start.10 = (bf16[8,4]{1,0:T(8,128)(2,1)S(1)}, bf16[8,4]{1,0:T(8,128)(2,1)S(1)}, u32[]{:S(2)}, u32[]{:S(2)}) collective-permute-start(bf16[8,4]{1,0:T(8,128)(2,1)S(1)} %get-tuple-element.108), channel_id=1, source_target_pairs={{0,1},{2,3},{4,5},{6,7},{8,9},{10,11},{12,13},{14,15},{16,17},{18,... | collective-permute-start | bytes 200 | tf_op jit(solution)/shard_map/ppermute | solution.py:15
  113.6 13.7 %collective-permute-start.11 = (bf16[8,4]{1,0:T(8,128)(2,1)S(1)}, bf16[8,4]{1,0:T(8,128)(2,1)S(1)}, u32[]{:S(2)}, u32[]{:S(2)}) collective-permute-start(bf16[8,4]{1,0:T(8,128)(2,1)S(1)} %get-tuple-element.109), channel_id=1, source_target_pairs={{1,0},{3,2},{5,4},{7,6},{9,8},{11,10},{13,12},{15,14},{17,16},{19,... | collective-permute-start | bytes 200 | tf_op jit(solution)/shard_map/ppermute | solution.py:15
  115.0 8.8 %collective-permute-start.5 = (bf16[4,16,1280]{2,1,0:T(8,128)(2,1)S(1)}, bf16[4,16,1280]{2,1,0:T(8,128)(2,1)S(1)}, u32[]{:S(2)}, u32[]{:S(2)}) collective-permute-start(bf16[4,16,1280]{2,1,0:T(8,128)(2,1)S(1)} %bitcast.45), channel_id=1, source_target_pairs={{2,0},{4,2},{6,4},{8,6},{10,8},{12,10},{14,12},{3,1},{5,3},{7,5},{... | collective-permute-start | bytes 491528 | tf_op jit(solution)/shard_map/ppermute | solution.py:15
  124.0 3.4 %collective-permute-start.6 = (bf16[8,4,1280]{2,1,0:T(4,128)(2,1)S(1)}, bf16[8,4,1280]{2,1,0:T(4,128)(2,1)S(1)}, u32[]{:S(2)}, u32[]{:S(2)}) collective-permute-start(bf16[8,4,1280]{2,1,0:T(4,128)(2,1)S(1)} %get-tuple-element.100), channel_id=1, source_target_pairs={{0,1},{2,3},{4,5},{6,7},{8,9},{10,11},{12,13},{14,15},{16,17},{18,... | collective-permute-start | bytes 245768 | tf_op jit(solution)/shard_map/ppermute | solution.py:15
  126.1 3.2 %collective-permute-start.7 = (bf16[8,4,1280]{2,1,0:T(4,128)(2,1)S(1)}, bf16[8,4,1280]{2,1,0:T(4,128)(2,1)S(1)}, u32[]{:S(2)}, u32[]{:S(2)}) collective-permute-start(bf16[8,4,1280]{2,1,0:T(4,128)(2,1)S(1)} %get-tuple-element.101), channel_id=1, source_target_pairs={{1,0},{3,2},{5,4},{7,6},{9,8},{11,10},{13,12},{15,14},{17,16},{19,... | collective-permute-start | bytes 245768 | tf_op jit(solution)/shard_map/ppermute | solution.py:15
Sparse Core Ops, SparseCore 0:
  9.5 56.8 all-gather.2
  68.5 38.4 all-gather.4
where the time goes:
time: 137 us
  waiting for transfers between devices  81.2 us (59%)
  starting transfers between devices  24.7 us (18%)
  between operations  13.7 us (10%)
  matrix products  10.6 us (8%)
  other arithmetic  3.6 us (3%)
  local copies, waits for them, and re-layouts  3.12 us (2%)
    all_gather x1, waiting for transfers between devices, body(): lax.all_gather(w_qkv, ('row', 'col'), axis=0, tiled=True)  37.5 us
    all_gather x1, waiting for transfers between devices, body(): lax.all_gather(w_out, ('row', 'col'), axis=0, tiled=True)  31.7 us
    ppermute x8, starting transfers between devices, shifted(): lax.ppermute(value, axis, [(source, source + steps) for source in range(i...  15.9 us
    ppermute x8, waiting for transfers between devices, shifted(): lax.ppermute(value, axis, [(source, source + steps) for source in range(i...  9.3 us
    ppermute x2, starting transfers between devices, extended(): lax.ppermute(lax.slice_in_dim(block, block.shape[dim] - width, None, axis...  6.17 us
    dot_general x1, matrix products, body(): jnp.dot(normed, lax.all_gather(w_qkv, ('row', 'col'), axis=0, tiled=True)...  4.14 us
  transfers between devices with their start and end apart: 14, of which 6 were waited for; matrix products, arithmetic and copies ran while one was open for 10% of the time, Pallas kernels for 0%

commit v1 on v0

--- a/solution.py
+++ b/solution.py
@@ -7,6 +7,24 @@
 EPSILON = 1e-06
 SPREAD = 4.0
 FLOOR = 0.25
+
+
+def gather_around(shard, axis, dim):
+    ways, here, step = (lax.axis_size(axis), lax.axis_index(axis), shard.shape[dim])
+    lengths = [n * ways if d == dim else n for d, n in enumerate(shard.shape)]
+    full = lax.dynamic_update_slice_in_dim(
+        jnp.zeros(lengths, shard.dtype), shard, here * step, axis=dim
+    )
+    going_up = going_down = shard
+    for far in range(1, ways // 2 + 1):
+        going_up = lax.ppermute(going_up, axis, [(d, (d + 1) % ways) for d in range(ways)])
+        full = lax.dynamic_update_slice_in_dim(full, going_up, (here - far) % ways * step, axis=dim)
+        if 2 * far < ways:
+            going_down = lax.ppermute(going_down, axis, [(d, (d - 1) % ways) for d in range(ways)])
+            full = lax.dynamic_update_slice_in_dim(
+                full, going_down, (here + far) % ways * step, axis=dim
+            )
+    return full
 
 
 def shifted(value, axis, steps):
@@ -112,7 +130,7 @@
     attended = jax.vmap(attend)(projected).reshape(tile_rows * rows_count, -1)
     projected_out = lax.dot_general(
         attended,
-        lax.all_gather(w_out, ("row", "col"), axis=0, tiled=True),
+        gather_around(w_out, ("row", "col"), 0),
         (((1,), (1,)), ((), ())),
         preferred_element_type=jnp.float32,
     )

time: 137 us -> 130 us (0.949)
  waiting for transfers between devices: 81.2 us -> 36.4 us
  starting transfers between devices: 24.7 us -> 57.4 us
  local copies, waits for them, and re-layouts: 3.12 us -> 7.55 us
    all_gather x1, waiting for transfers between devices: 37.5 us -> 0.02 us  [body(): lax.all_gather(w_qkv, ('row', 'col'), axis=0, tiled=True)]
    ppermute x0 -> x15, starting transfers between devices: none -> 33 us  [the longest x7 32.4 us: gather_around(): lax.ppermute(going_down, axis, [(d, (d - 1) % ways) for d in range(ways)])]
    all_gather x1 -> x0, waiting for transfers between devices: 31.7 us -> none  [body(): lax.all_gather(w_out, ('row', 'col'), axis=0, tiled=True)]
    ppermute x0 -> x15, waiting for transfers between devices: none -> 23.7 us  [the longest x8 15.5 us: gather_around(): lax.ppermute(going_up, axis, [(d, (d + 1) % ways) for d in range(ways)])]
    ppermute x8, waiting for transfers between devices: 9.3 us -> 11.9 us  [shifted(): lax.ppermute(value, axis, [(source, source + steps) for source in range(i...]
    ppermute x2, waiting for transfers between devices: 1.92 us -> 0.01 us  [extended(): lax.ppermute(lax.slice_in_dim(block, 0, width, axis=dim), axis, backward)]
    ppermute x2, starting transfers between devices: 6.17 us -> 4.34 us  [extended(): lax.ppermute(lax.slice_in_dim(block, block.shape[dim] - width, None, axis...]
    slice x1, local copies, waits for them, and re-layouts: 0.19 us -> 1.88 us  [attend(): queries = projected[:, :width].reshape(rows_count, HEADS, head_size)]
  transfers between devices with their start and end apart: 14 -> 28, of which waited for: 6 -> 16; matrix products, arithmetic and copies ran while one was open for 10% -> 4% of each run, Pallas kernels for 0% -> 0%
where the time goes in v1:
time: 130 us; the launch traced here: 129 us
  starting transfers between devices  57.4 us (44%)
  waiting for transfers between devices  36.4 us (28%)
  between operations  14.2 us (11%)
  matrix products  10.1 us (8%)
  local copies, waits for them, and re-layouts  7.55 us (6%)
  other arithmetic  3.53 us (3%)
    ppermute x7, starting transfers between devices, gather_around(): lax.ppermute(going_down, axis, [(d, (d - 1) % ways) for d in range(ways)])  32.4 us
    ppermute x8, starting transfers between devices, shifted(): lax.ppermute(value, axis, [(source, source + steps) for source in range(i...  17.3 us
    ppermute x8, waiting for transfers between devices, gather_around(): lax.ppermute(going_up, axis, [(d, (d + 1) % ways) for d in range(ways)])  15.5 us
    ppermute x8, waiting for transfers between devices, shifted(): lax.ppermute(value, axis, [(source, source + steps) for source in range(i...  11.9 us
    ppermute x7, waiting for transfers between devices, gather_around(): lax.ppermute(going_down, axis, [(d, (d - 1) % ways) for d in range(ways)])  8.22 us
    ppermute x2, starting transfers between devices, extended(): lax.ppermute(lax.slice_in_dim(block, block.shape[dim] - width, None, axis...  4.34 us
    dot_general x1, matrix products, body(): jnp.dot(normed, lax.all_gather(w_qkv, ('row', 'col'), axis=0, tiled=True)...  4.1 us
    sub x1, matrix products, attend(): expon = jnp.exp(scores - highest)  3.31 us
  transfers between devices with their start and end apart: 28, of which 16 were waited for; matrix products, arithmetic and copies ran while one was open for 4% of the time, Pallas kernels for 0%

profile of v1, /device:TPU:0, one launch (start us, length us, event | category | flops | bytes accessed | tf_op | source)
XLA Modules:
  0.0 129.2 jit_solution(5375665522742085773)
XLA Ops:
  7.8 5.0 %collective-permute-start.5 = (bf16[80,640]{1,0:T(8,128)(2,1)}, bf16[80,640]{1,0:T(8,128)(2,1)S(1)}, u32[]{:S(2)}, u32[]{:S(2)}) collective-permute-start(bf16[80,640]{1,0:T(8,128)(2,1)} %param.31), channel_id=1, source_target_pairs={{0,15},{1,0},{2,1},{3,2},{4,3},{5,4},{6,5},{7,6},{8,7},{9,8},{10,9... | collective-permute-start | bytes 307208 | tf_op jit(solution)/shard_map/ppermute | solution.py:23
  17.3 4.8 %collective-permute-start.23 = (bf16[4,16]{1,0:T(4,128)(2,1)S(1)}, bf16[4,16]{1,0:T(4,128)(2,1)S(1)}, u32[]{:S(2)}, u32[]{:S(2)}) collective-permute-start(bf16[4,16]{1,0:T(4,128)(2,1)S(1)} %get-tuple-element.107), channel_id=1, source_target_pairs={{0,2},{2,4},{4,6},{6,8},{8,10},{10,12},{12,14},{1,3},{3,5},{5,7},{... | collective-permute-start | bytes 392 | tf_op jit(solution)/shard_map/ppermute | solution.py:33
  24.7 5.1 %collective-permute-done.24 = bf16[4,16]{1,0:T(4,128)(2,1)S(1)} collective-permute-done((bf16[4,16]{1,0:T(4,128)(2,1)S(1)}, bf16[4,16]{1,0:T(4,128)(2,1)S(1)}, u32[]{:S(2)}, u32[]{:S(2)}) %collective-permute-start.24) | collective-permute-done | bytes 160 | tf_op jit(solution)/shard_map/ppermute | solution.py:33
  31.4 3.0 %collective-permute-start.2 = (bf16[16,4,1280]{2,1,0:T(4,128)(2,1)S(1)}, bf16[16,4,1280]{2,1,0:T(4,128)(2,1)S(1)}, u32[]{:S(2)}, u32[]{:S(2)}) collective-permute-start(bf16[16,4,1280]{2,1,0:T(4,128)(2,1)S(1)} %get-tuple-element.102), channel_id=1, source_target_pairs={{0,1},{2,3},{4,5},{6,7},{8,9},{10,11},{12,13},{14,15},{16,17},{18,... | collective-permute-start | bytes 491528 | tf_op jit(solution)/shard_map/ppermute | solution.py:41
  34.6 4.4 %collective-permute-start.7 = (bf16[80,640]{1,0:T(8,128)(2,1)S(1)}, bf16[80,640]{1,0:T(8,128)(2,1)S(1)}, u32[]{:S(2)}, u32[]{:S(2)}) collective-permute-start(bf16[80,640]{1,0:T(8,128)(2,1)S(1)} %collective-permute-done.5), channel_id=1, source_target_pairs={{0,15},{1,0},{2,1},{3,2},{4,3},{5,4},{6,5},{7,6},{8,7},{9,8},{10,9... | collective-permute-start | bytes 307208 | tf_op jit(solution)/shard_map/ppermute | solution.py:23
  39.0 2.3 %collective-permute-done.6 = bf16[80,640]{1,0:T(8,128)(2,1)S(1)} collective-permute-done((bf16[80,640]{1,0:T(8,128)(2,1)S(1)}, bf16[80,640]{1,0:T(8,128)(2,1)S(1)}, u32[]{:S(2)}, u32[]{:S(2)}) %collective-permute-start.6) | collective-permute-done | bytes 102432 | tf_op jit(solution)/shard_map/ppermute | solution.py:20
  41.4 1.8 %collective-permute-done.7 = bf16[80,640]{1,0:T(8,128)(2,1)S(1)} collective-permute-done((bf16[80,640]{1,0:T(8,128)(2,1)S(1)}, bf16[80,640]{1,0:T(8,128)(2,1)S(1)}, u32[]{:S(2)}, u32[]{:S(2)}) %collective-permute-start.7) | collective-permute-done | bytes 102432 | tf_op jit(solution)/shard_map/ppermute | solution.py:23
  43.2 4.6 %collective-permute-start.9 = (bf16[80,640]{1,0:T(8,128)(2,1)S(1)}, bf16[80,640]{1,0:T(8,128)(2,1)S(1)}, u32[]{:S(2)}, u32[]{:S(2)}) collective-permute-start(bf16[80,640]{1,0:T(8,128)(2,1)S(1)} %collective-permute-done.7), channel_id=1, source_target_pairs={{0,15},{1,0},{2,1},{3,2},{4,3},{5,4},{6,5},{7,6},{8,7},{9,8},{10,9... | collective-permute-start | bytes 307208 | tf_op jit(solution)/shard_map/ppermute | solution.py:23
  51.9 4.6 %collective-permute-start.11 = (bf16[80,640]{1,0:T(8,128)(2,1)S(1)}, bf16[80,640]{1,0:T(8,128)(2,1)S(1)}, u32[]{:S(2)}, u32[]{:S(2)}) collective-permute-start(bf16[80,640]{1,0:T(8,128)(2,1)S(1)} %collective-permute-done.9), channel_id=1, source_target_pairs={{0,15},{1,0},{2,1},{3,2},{4,3},{5,4},{6,5},{7,6},{8,7},{9,8},{10,9... | collective-permute-start | bytes 307208 | tf_op jit(solution)/shard_map/ppermute | solution.py:23
  56.5 1.8 %collective-permute-done.10 = bf16[80,640]{1,0:T(8,128)(2,1)S(1)} collective-permute-done((bf16[80,640]{1,0:T(8,128)(2,1)S(1)}, bf16[80,640]{1,0:T(8,128)(2,1)S(1)}, u32[]{:S(2)}, u32[]{:S(2)}) %collective-permute-start.10) | collective-permute-done | bytes 102432 | tf_op jit(solution)/shard_map/ppermute | solution.py:20
  58.7 4.6 %collective-permute-start.13 = (bf16[80,640]{1,0:T(8,128)(2,1)S(1)}, bf16[80,640]{1,0:T(8,128)(2,1)S(1)}, u32[]{:S(2)}, u32[]{:S(2)}) collective-permute-start(bf16[80,640]{1,0:T(8,128)(2,1)S(1)} %collective-permute-done.11), channel_id=1, source_target_pairs={{0,15},{1,0},{2,1},{3,2},{4,3},{5,4},{6,5},{7,6},{8,7},{9,8},{10,9... | collective-permute-start | bytes 307208 | tf_op jit(solution)/shard_map/ppermute | solution.py:23
  63.4 1.9 %collective-permute-done.12 = bf16[80,640]{1,0:T(8,128)(2,1)S(1)} collective-permute-done((bf16[80,640]{1,0:T(8,128)(2,1)S(1)}, bf16[80,640]{1,0:T(8,128)(2,1)S(1)}, u32[]{:S(2)}, u32[]{:S(2)}) %collective-permute-start.12) | collective-permute-done | bytes 102432 | tf_op jit(solution)/shard_map/ppermute | solution.py:20
  65.4 2.4 %collective-permute-done.13 = bf16[80,640]{1,0:T(8,128)(2,1)S(1)} collective-permute-done((bf16[80,640]{1,0:T(8,128)(2,1)S(1)}, bf16[80,640]{1,0:T(8,128)(2,1)S(1)}, u32[]{:S(2)}, u32[]{:S(2)}) %collective-permute-start.13) | collective-permute-done | bytes 102432 | tf_op jit(solution)/shard_map/ppermute | solution.py:23
  67.8 4.6 %collective-permute-start.15 = (bf16[80,640]{1,0:T(8,128)(2,1)S(1)}, bf16[80,640]{1,0:T(8,128)(2,1)S(1)}, u32[]{:S(2)}, u32[]{:S(2)}) collective-permute-start(bf16[80,640]{1,0:T(8,128)(2,1)S(1)} %collective-permute-done.13), channel_id=1, source_target_pairs={{0,15},{1,0},{2,1},{3,2},{4,3},{5,4},{6,5},{7,6},{8,7},{9,8},{10,9... | collective-permute-start | bytes 307208 | tf_op jit(solution)/shard_map/ppermute | solution.py:23
  74.6 4.5 %collective-permute-start.17 = (bf16[80,640]{1,0:T(8,128)(2,1)S(1)}, bf16[80,640]{1,0:T(8,128)(2,1)S(1)}, u32[]{:S(2)}, u32[]{:S(2)}) collective-permute-start(bf16[80,640]{1,0:T(8,128)(2,1)S(1)} %collective-permute-done.15), channel_id=1, source_target_pairs={{0,15},{1,0},{2,1},{3,2},{4,3},{5,4},{6,5},{7,6},{8,7},{9,8},{10,9... | collective-permute-start | bytes 307208 | tf_op jit(solution)/shard_map/ppermute | solution.py:23
  81.5 5.6 %collective-permute-done.18 = bf16[80,640]{1,0:T(8,128)(2,1)S(1)} collective-permute-done((bf16[80,640]{1,0:T(8,128)(2,1)S(1)}, bf16[80,640]{1,0:T(8,128)(2,1)S(1)}, u32[]{:S(2)}, u32[]{:S(2)}) %collective-permute-start.18) | collective-permute-done | bytes 102432 | tf_op jit(solution)/shard_map/ppermute | solution.py:20
  87.1 4.1 %fusion.4 = bf16[1,256,1920]{2,1,0:T(8,128)(2,1)S(1)} fusion(bf16[1280,1920]{1,0:T(8,128)(2,1)} %all-gather.2.cloned.1.call-done, f32[1920]{0:T(1024)S(1)} %copy-done.5, bf16[256,1280]{1,0:T(8,128)(2,1)S(1)} %copy-done, bf16[256,1280]{1,0:T(8,128)(2,1)S(1)} %bitcast.37, f32[1280]{0:T(1024)S(1)} %copy-done.6, f32[1280]{0:T(1024)S(1)} %copy-done.7, ...), kind=kOutput, calls=%fused_computation.6 | convolution fusion | flops 1261895680 | bytes 7228928 | tf_op jit(solution)/shard_map/dot_general | solution.py:122
  92.2 1.9 %copy.14 = bf16[1,256,640]{1,2,0:T(8,128)(2,1)} copy(bf16[1,256,640]{2,1,0:T(8,128)(2,1)} %get-tuple-element.97) | data formatting | bytes 655360 | tf_op jit(solution)/shard_map/vmap()/slice | solution.py:67
  94.0 1.9 %copy.15 = bf16[1,256,640]{1,2,0:T(8,128)(2,1)} copy(bf16[1,256,640]{2,1,0:T(8,128)(2,1)} %get-tuple-element.96) | data formatting | bytes 655360 | tf_op jit(solution)/shard_map/vmap()/slice | solution.py:65
  96.8 3.3 %fusion.26 = (f32[8,256]{1,0:T(8,128)S(1)}, f32[8,256,256]{1,2,0:T(8,128)}) fusion(bf16[256,8,80]{0,2,1:T(8,128)(2,1)} %bitcast.43, bf16[256,8,80]{0,2,1:T(8,128)(2,1)} %bitcast.44), kind=kOutput, calls=%fused_computation.71 | convolution fusion | flops 85459200 | bytes 2760704 | tf_op jit(solution)/shard_map/vmap()/sub | solution.py:72
  100.1 1.9 %convolution_convert_fusion = bf16[8,80,256]{2,1,0:T(8,128)(2,1)S(1)} fusion(bf16[256,8,80]{0,2,1:T(8,128)(2,1)S(1)} %bitcast.42, f32[8,256,256]{1,2,0:T(8,128)} %get-tuple-element.111, f32[8,256]{1,0:T(8,128)S(1)} %get-tuple-element.110), kind=kOutput, calls=%fused_computation.14 | convolution fusion | flops 85098496 | bytes 2760704 | tf_op jit(solution)/shard_map/vmap(hqk,khd->qhd)/dot_general | solution.py:74
  105.6 3.0 %collective-permute-start.25 = (bf16[8,4]{1,0:T(8,128)(2,1)S(1)}, bf16[8,4]{1,0:T(8,128)(2,1)S(1)}, u32[]{:S(2)}, u32[]{:S(2)}) collective-permute-start(bf16[8,4]{1,0:T(8,128)(2,1)S(1)} %get-tuple-element.108), channel_id=1, source_target_pairs={{0,1},{2,3},{4,5},{6,7},{8,9},{10,11},{12,13},{14,15},{16,17},{18,... | collective-permute-start | bytes 200 | tf_op jit(solution)/shard_map/ppermute | solution.py:33
  110.1 6.0 %collective-permute-done.20 = bf16[4,16,1280]{2,1,0:T(8,128)(2,1)S(1)} collective-permute-done((bf16[4,16,1280]{2,1,0:T(8,128)(2,1)S(1)}, bf16[4,16,1280]{2,1,0:T(8,128)(2,1)S(1)}, u32[]{:S(2)}, u32[]{:S(2)}) %collective-permute-start.20) | collective-permute-done | bytes 163872 | tf_op jit(solution)/shard_map/ppermute | solution.py:33
  117.6 3.0 %collective-permute-start.21 = (bf16[8,4,1280]{2,1,0:T(4,128)(2,1)S(1)}, bf16[8,4,1280]{2,1,0:T(4,128)(2,1)S(1)}, u32[]{:S(2)}, u32[]{:S(2)}) collective-permute-start(bf16[8,4,1280]{2,1,0:T(4,128)(2,1)S(1)} %get-tuple-element.100), channel_id=1, source_target_pairs={{0,1},{2,3},{4,5},{6,7},{8,9},{10,11},{12,13},{14,15},{16,17},{18,... | collective-permute-start | bytes 245768 | tf_op jit(solution)/shard_map/ppermute | solution.py:33
  (107 shorter events, 28.5 us)
Async XLA Ops:
  6.5 80.6 %all-gather.2.cloned.1.call-start = ((), (), s32[]{:S(2)}) async-start(), calls=%async_computation | async-start | bytes 5222400 | tf_op jit(solution)/shard_map/all_gather | solution.py:124
  7.3 27.2 %collective-permute-start.4 = (bf16[80,640]{1,0:T(8,128)(2,1)}, bf16[80,640]{1,0:T(8,128)(2,1)S(1)}, u32[]{:S(2)}, u32[]{:S(2)}) collective-permute-start(bf16[80,640]{1,0:T(8,128)(2,1)} %param.31), channel_id=1, source_target_pairs={{0,1},{1,2},{2,3},{3,4},{4,5},{5,6},{6,7},{7,8},{8,9},{9,10},{10,1... | collective-permute-start | bytes 307208 | tf_op jit(solution)/shard_map/ppermute | solution.py:20
  7.8 26.8 %collective-permute-start.5 = (bf16[80,640]{1,0:T(8,128)(2,1)}, bf16[80,640]{1,0:T(8,128)(2,1)S(1)}, u32[]{:S(2)}, u32[]{:S(2)}) collective-permute-start(bf16[80,640]{1,0:T(8,128)(2,1)} %param.31), channel_id=1, source_target_pairs={{0,15},{1,0},{2,1},{3,2},{4,3},{5,4},{6,5},{7,6},{8,7},{9,8},{10,9... | collective-permute-start | bytes 307208 | tf_op jit(solution)/shard_map/ppermute | solution.py:23
  13.8 16.0 %collective-permute-start = (bf16[4,8,1280]{2,1,0:T(8,128)(2,1)S(1)}, bf16[4,8,1280]{2,1,0:T(8,128)(2,1)S(1)}, u32[]{:S(2)}, u32[]{:S(2)}) collective-permute-start(bf16[4,8,1280]{2,1,0:T(8,128)(2,1)S(1)} %get-tuple-element.105), channel_id=1, source_target_pairs={{0,2},{2,4},{4,6},{6,8},{8,10},{10,12},{12,14},{1,3},{3,5},{5,7},{... | collective-permute-start | bytes 245768 | tf_op jit(solution)/shard_map/ppermute | solution.py:41
  15.1 14.8 %collective-permute-start.1 = (bf16[4,8,1280]{2,1,0:T(8,128)(2,1)S(1)}, bf16[4,8,1280]{2,1,0:T(8,128)(2,1)S(1)}, u32[]{:S(2)}, u32[]{:S(2)}) collective-permute-start(bf16[4,8,1280]{2,1,0:T(8,128)(2,1)S(1)} %get-tuple-element.104), channel_id=1, source_target_pairs={{2,0},{4,2},{6,4},{8,6},{10,8},{12,10},{14,12},{3,1},{5,3},{7,5},{... | collective-permute-start | bytes 245768 | tf_op jit(solution)/shard_map/ppermute | solution.py:44
  30.0 17.8 %collective-permute-start.3 = (bf16[16,4,1280]{2,1,0:T(4,128)(2,1)S(1)}, bf16[16,4,1280]{2,1,0:T(4,128)(2,1)S(1)}, u32[]{:S(2)}, u32[]{:S(2)}) collective-permute-start(bf16[16,4,1280]{2,1,0:T(4,128)(2,1)S(1)} %get-tuple-element.103), channel_id=1, source_target_pairs={{1,0},{3,2},{5,4},{7,6},{9,8},{11,10},{13,12},{15,14},{17,16},{19,... | collective-permute-start | bytes 491528 | tf_op jit(solution)/shard_map/ppermute | solution.py:44
  31.4 16.4 %collective-permute-start.2 = (bf16[16,4,1280]{2,1,0:T(4,128)(2,1)S(1)}, bf16[16,4,1280]{2,1,0:T(4,128)(2,1)S(1)}, u32[]{:S(2)}, u32[]{:S(2)}) collective-permute-start(bf16[16,4,1280]{2,1,0:T(4,128)(2,1)S(1)} %get-tuple-element.102), channel_id=1, source_target_pairs={{0,1},{2,3},{4,5},{6,7},{8,9},{10,11},{12,13},{14,15},{16,17},{18,... | collective-permute-start | bytes 491528 | tf_op jit(solution)/shard_map/ppermute | solution.py:41
  34.5 6.9 %collective-permute-start.6 = (bf16[80,640]{1,0:T(8,128)(2,1)S(1)}, bf16[80,640]{1,0:T(8,128)(2,1)S(1)}, u32[]{:S(2)}, u32[]{:S(2)}) collective-permute-start(bf16[80,640]{1,0:T(8,128)(2,1)S(1)} %collective-permute-done.4), channel_id=1, source_target_pairs={{0,1},{1,2},{2,3},{3,4},{4,5},{5,6},{6,7},{7,8},{8,9},{9,10},{10,1... | collective-permute-start | bytes 307208 | tf_op jit(solution)/shard_map/ppermute | solution.py:20
  34.6 8.6 %collective-permute-start.7 = (bf16[80,640]{1,0:T(8,128)(2,1)S(1)}, bf16[80,640]{1,0:T(8,128)(2,1)S(1)}, u32[]{:S(2)}, u32[]{:S(2)}) collective-permute-start(bf16[80,640]{1,0:T(8,128)(2,1)S(1)} %collective-permute-done.5), channel_id=1, source_target_pairs={{0,15},{1,0},{2,1},{3,2},{4,3},{5,4},{6,5},{7,6},{8,7},{9,8},{10,9... | collective-permute-start | bytes 307208 | tf_op jit(solution)/shard_map/ppermute | solution.py:23
  41.4 9.1 %collective-permute-start.8 = (bf16[80,640]{1,0:T(8,128)(2,1)S(1)}, bf16[80,640]{1,0:T(8,128)(2,1)S(1)}, u32[]{:S(2)}, u32[]{:S(2)}) collective-permute-start(bf16[80,640]{1,0:T(8,128)(2,1)S(1)} %collective-permute-done.6), channel_id=1, source_target_pairs={{0,1},{1,2},{2,3},{3,4},{4,5},{5,6},{6,7},{7,8},{8,9},{9,10},{10,1... | collective-permute-start | bytes 307208 | tf_op jit(solution)/shard_map/ppermute | solution.py:20
  43.2 8.7 %collective-permute-start.9 = (bf16[80,640]{1,0:T(8,128)(2,1)S(1)}, bf16[80,640]{1,0:T(8,128)(2,1)S(1)}, u32[]{:S(2)}, u32[]{:S(2)}) collective-permute-start(bf16[80,640]{1,0:T(8,128)(2,1)S(1)} %collective-permute-done.7), channel_id=1, source_target_pairs={{0,15},{1,0},{2,1},{3,2},{4,3},{5,4},{6,5},{7,6},{8,7},{9,8},{10,9... | collective-permute-start | bytes 307208 | tf_op jit(solution)/shard_map/ppermute | solution.py:23
  50.5 7.9 %collective-permute-start.10 = (bf16[80,640]{1,0:T(8,128)(2,1)S(1)}, bf16[80,640]{1,0:T(8,128)(2,1)S(1)}, u32[]{:S(2)}, u32[]{:S(2)}) collective-permute-start(bf16[80,640]{1,0:T(8,128)(2,1)S(1)} %collective-permute-done.8), channel_id=1, source_target_pairs={{0,1},{1,2},{2,3},{3,4},{4,5},{5,6},{6,7},{7,8},{8,9},{9,10},{10,1... | collective-permute-start | bytes 307208 | tf_op jit(solution)/shard_map/ppermute | solution.py:20
  51.9 6.9 %collective-permute-start.11 = (bf16[80,640]{1,0:T(8,128)(2,1)S(1)}, bf16[80,640]{1,0:T(8,128)(2,1)S(1)}, u32[]{:S(2)}, u32[]{:S(2)}) collective-permute-start(bf16[80,640]{1,0:T(8,128)(2,1)S(1)} %collective-permute-done.9), channel_id=1, source_target_pairs={{0,15},{1,0},{2,1},{3,2},{4,3},{5,4},{6,5},{7,6},{8,7},{9,8},{10,9... | collective-permute-start | bytes 307208 | tf_op jit(solution)/shard_map/ppermute | solution.py:23
  58.4 7.0 %collective-permute-start.12 = (bf16[80,640]{1,0:T(8,128)(2,1)S(1)}, bf16[80,640]{1,0:T(8,128)(2,1)S(1)}, u32[]{:S(2)}, u32[]{:S(2)}) collective-permute-start(bf16[80,640]{1,0:T(8,128)(2,1)S(1)} %collective-permute-done.10), channel_id=1, source_target_pairs={{0,1},{1,2},{2,3},{3,4},{4,5},{5,6},{6,7},{7,8},{8,9},{9,10},{10,1... | collective-permute-start | bytes 307208 | tf_op jit(solution)/shard_map/ppermute | solution.py:20
  58.7 9.1 %collective-permute-start.13 = (bf16[80,640]{1,0:T(8,128)(2,1)S(1)}, bf16[80,640]{1,0:T(8,128)(2,1)S(1)}, u32[]{:S(2)}, u32[]{:S(2)}) collective-permute-start(bf16[80,640]{1,0:T(8,128)(2,1)S(1)} %collective-permute-done.11), channel_id=1, source_target_pairs={{0,15},{1,0},{2,1},{3,2},{4,3},{5,4},{6,5},{7,6},{8,7},{9,8},{10,9... | collective-permute-start | bytes 307208 | tf_op jit(solution)/shard_map/ppermute | solution.py:23
  65.3 8.2 %collective-permute-start.14 = (bf16[80,640]{1,0:T(8,128)(2,1)S(1)}, bf16[80,640]{1,0:T(8,128)(2,1)S(1)}, u32[]{:S(2)}, u32[]{:S(2)}) collective-permute-start(bf16[80,640]{1,0:T(8,128)(2,1)S(1)} %collective-permute-done.12), channel_id=1, source_target_pairs={{0,1},{1,2},{2,3},{3,4},{4,5},{5,6},{6,7},{7,8},{8,9},{9,10},{10,1... | collective-permute-start | bytes 307208 | tf_op jit(solution)/shard_map/ppermute | solution.py:20
  67.8 6.9 %collective-permute-start.15 = (bf16[80,640]{1,0:T(8,128)(2,1)S(1)}, bf16[80,640]{1,0:T(8,128)(2,1)S(1)}, u32[]{:S(2)}, u32[]{:S(2)}) collective-permute-start(bf16[80,640]{1,0:T(8,128)(2,1)S(1)} %collective-permute-done.13), channel_id=1, source_target_pairs={{0,15},{1,0},{2,1},{3,2},{4,3},{5,4},{6,5},{7,6},{8,7},{9,8},{10,9... | collective-permute-start | bytes 307208 | tf_op jit(solution)/shard_map/ppermute | solution.py:23
  73.5 6.8 %collective-permute-start.16 = (bf16[80,640]{1,0:T(8,128)(2,1)S(1)}, bf16[80,640]{1,0:T(8,128)(2,1)S(1)}, u32[]{:S(2)}, u32[]{:S(2)}) collective-permute-start(bf16[80,640]{1,0:T(8,128)(2,1)S(1)} %collective-permute-done.14), channel_id=1, source_target_pairs={{0,1},{1,2},{2,3},{3,4},{4,5},{5,6},{6,7},{7,8},{8,9},{9,10},{10,1... | collective-permute-start | bytes 307208 | tf_op jit(solution)/shard_map/ppermute | solution.py:20
  74.6 6.8 %collective-permute-start.17 = (bf16[80,640]{1,0:T(8,128)(2,1)S(1)}, bf16[80,640]{1,0:T(8,128)(2,1)S(1)}, u32[]{:S(2)}, u32[]{:S(2)}) collective-permute-start(bf16[80,640]{1,0:T(8,128)(2,1)S(1)} %collective-permute-done.15), channel_id=1, source_target_pairs={{0,15},{1,0},{2,1},{3,2},{4,3},{5,4},{6,5},{7,6},{8,7},{9,8},{10,9... | collective-permute-start | bytes 307208 | tf_op jit(solution)/shard_map/ppermute | solution.py:23
  80.3 6.8 %collective-permute-start.18 = (bf16[80,640]{1,0:T(8,128)(2,1)S(1)}, bf16[80,640]{1,0:T(8,128)(2,1)S(1)}, u32[]{:S(2)}, u32[]{:S(2)}) collective-permute-start(bf16[80,640]{1,0:T(8,128)(2,1)S(1)} %collective-permute-done.16), channel_id=1, source_target_pairs={{0,1},{1,2},{2,3},{3,4},{4,5},{5,6},{6,7},{7,8},{8,9},{9,10},{10,1... | collective-permute-start | bytes 307208 | tf_op jit(solution)/shard_map/ppermute | solution.py:20
  102.9 7.1 %collective-permute-start.19 = (bf16[4,16,1280]{2,1,0:T(8,128)(2,1)S(1)}, bf16[4,16,1280]{2,1,0:T(8,128)(2,1)S(1)}, u32[]{:S(2)}, u32[]{:S(2)}) collective-permute-start(bf16[4,16,1280]{2,1,0:T(8,128)(2,1)S(1)} %bitcast.46), channel_id=1, source_target_pairs={{0,2},{2,4},{4,6},{6,8},{8,10},{10,12},{12,14},{1,3},{3,5},{5,7},{... | collective-permute-start | bytes 491528 | tf_op jit(solution)/shard_map/ppermute | solution.py:33
  104.3 16.3 %collective-permute-start.26 = (bf16[8,4]{1,0:T(8,128)(2,1)S(1)}, bf16[8,4]{1,0:T(8,128)(2,1)S(1)}, u32[]{:S(2)}, u32[]{:S(2)}) collective-permute-start(bf16[8,4]{1,0:T(8,128)(2,1)S(1)} %get-tuple-element.109), channel_id=1, source_target_pairs={{1,0},{3,2},{5,4},{7,6},{9,8},{11,10},{13,12},{15,14},{17,16},{19,... | collective-permute-start | bytes 200 | tf_op jit(solution)/shard_map/ppermute | solution.py:33
  105.6 15.1 %collective-permute-start.25 = (bf16[8,4]{1,0:T(8,128)(2,1)S(1)}, bf16[8,4]{1,0:T(8,128)(2,1)S(1)}, u32[]{:S(2)}, u32[]{:S(2)}) collective-permute-start(bf16[8,4]{1,0:T(8,128)(2,1)S(1)} %get-tuple-element.108), channel_id=1, source_target_pairs={{0,1},{2,3},{4,5},{6,7},{8,9},{10,11},{12,13},{14,15},{16,17},{18,... | collective-permute-start | bytes 200 | tf_op jit(solution)/shard_map/ppermute | solution.py:33
  108.7 7.4 %collective-permute-start.20 = (bf16[4,16,1280]{2,1,0:T(8,128)(2,1)S(1)}, bf16[4,16,1280]{2,1,0:T(8,128)(2,1)S(1)}, u32[]{:S(2)}, u32[]{:S(2)}) collective-permute-start(bf16[4,16,1280]{2,1,0:T(8,128)(2,1)S(1)} %bitcast.45), channel_id=1, source_target_pairs={{2,0},{4,2},{6,4},{8,6},{10,8},{12,10},{14,12},{3,1},{5,3},{7,5},{... | collective-permute-start | bytes 491528 | tf_op jit(solution)/shard_map/ppermute | solution.py:33
  (12 other events, 200.6 us)
Sparse Core Ops, SparseCore 0:
  9.5 63.9 all-gather.1
